TPU v7x, 32 devices: a whole 2x2x4 slice. The times are simulated.
32 devices in a mesh: cand: 4 (over x, core), seq: 8 (over z, y).
Axes of the slice: x: 2, y: 2, z: 4, core: 2. Of those that a mesh axis runs over, the one named last changes fastest.
Arguments:
- response_query_array: bfloat16 [8, 768, 2560], P('cand', 'seq'), may hold values from -180 to 180
- response_key_array: bfloat16 [8, 768, 512], P('cand', 'seq'), may hold values from -6 to 6
- response_value_array: bfloat16 [8, 768, 512], P('cand', 'seq'), may hold values from -6 to 6
- prompt_key_array: bfloat16 [2048, 512], P(('cand', 'seq')), may hold values from -6 to 6
- prompt_value_array: bfloat16 [2048, 512], P(('cand', 'seq')), may hold values from -6 to 6
- lengths: int32 [8], replicated, may hold values from 192 to 768, as said below
- offsets: int32 [8], replicated, may hold values from 512 to 2048, as said below
- ranks: int32 [8], replicated, may hold values from 0 to 7, each once
Outputs:
- attention: bfloat16 [8, 768, 2560], P('cand', 'seq')
Inputs may be any that keep to these rules, and one draw needn't show every extreme that they name: `lengths`: some candidate's response has all 768 positions live. `offsets`: some candidate sees the whole prompt.
All inputs are finite; a program needn't handle non-finite values.
Results may differ from a plain program's by a relative error of at most 0.004.
Values may be sent and summed in bfloat16 or wider, within the bound.
No kernel may reach another device: no remote copies, remote signals or barrier semaphores. Data moves between devices by JAX's collectives and lax.ppermute only.
A program may use at most 128 MiB of HBM per device.

v0:
```python
import math
import jax
import jax.numpy as jnp
from jax import lax
from jax.sharding import PartitionSpec as P

QUERY_HEADS = 20
KEY_VALUE_HEADS = 4
HEAD_DIMENSION = 128
lowest_score_value = -1e30


def attend_block(running, query_rows, block_keys, block_values, allowed, shared):
    running_max, running_total, running_sum = running
    cand_count = query_rows.shape[0]
    heads_kv = query_rows.shape[2]
    head_size = query_rows.shape[4]
    score_scale = 1.0 / math.sqrt(head_size)
    if shared:
        keys_split = block_keys.reshape(block_keys.shape[0], heads_kv, head_size)
        values_split = block_values.reshape(block_values.shape[0], heads_kv, head_size)
        scores = jnp.einsum(
            "crhgd,nhd->chgrn", query_rows, keys_split, preferred_element_type=jnp.float32
        )
    else:
        keys_split = block_keys.reshape(cand_count, block_keys.shape[1], heads_kv, head_size)
        values_split = block_values.reshape(cand_count, block_values.shape[1], heads_kv, head_size)
        scores = jnp.einsum(
            "crhgd,cnhd->chgrn", query_rows, keys_split, preferred_element_type=jnp.float32
        )
    scores = jnp.where(allowed[:, None, None, :, :], scores * score_scale, -jnp.inf)
    new_max = jnp.maximum(running_max, jnp.max(scores, axis=-1))
    rescale = jnp.exp(running_max - new_max)
    exponent = jnp.exp(scores - new_max[..., None])
    weights = exponent.astype(jnp.bfloat16)
    new_total = running_total * rescale + jnp.sum(exponent, axis=-1)
    if shared:
        contrib = jnp.einsum(
            "chgrn,nhd->chgrd", weights, values_split, preferred_element_type=jnp.float32
        )
    else:
        contrib = jnp.einsum(
            "chgrn,cnhd->chgrd", weights, values_split, preferred_element_type=jnp.float32
        )
    new_sum = running_sum * rescale[..., None] + contrib
    return (new_max, new_total, new_sum)


def fold_blocks(
    running, query_rows, all_keys, all_values, key_pos, allowed_of, shared, live_of=None
):
    key_count = key_pos.shape[0]
    block_len = math.gcd(key_count, 512)
    keys_axis = 0 if shared else 1

    def one_block(step_at, carried):
        block_start = step_at * block_len
        block_keys = lax.dynamic_slice_in_dim(all_keys, block_start, block_len, keys_axis)
        block_values = lax.dynamic_slice_in_dim(all_values, block_start, block_len, keys_axis)
        block_pos = lax.dynamic_slice_in_dim(key_pos, block_start, block_len, 0)
        return attend_block(
            carried, query_rows, block_keys, block_values, allowed_of(block_pos), shared
        )

    return lax.fori_loop(0, key_count // block_len, one_block, running)


def body(
    response_query_array,
    response_key_array,
    response_value_array,
    prompt_key_array,
    prompt_value_array,
    lengths,
    offsets,
    ranks,
):
    candidate_local, output_rows, width = response_query_array.shape
    group_width = QUERY_HEADS // KEY_VALUE_HEADS
    group_at = lax.axis_index("cand")
    seq_at = lax.axis_index("seq")
    first_cand = group_at * candidate_local
    my_lengths = lax.dynamic_slice_in_dim(lengths, first_cand, candidate_local)
    my_offsets = lax.dynamic_slice_in_dim(offsets, first_cand, candidate_local)
    query_pos = seq_at * output_rows + jnp.arange(output_rows, dtype=jnp.int32)
    query_rows = response_query_array.reshape(
        candidate_local, output_rows, KEY_VALUE_HEADS, group_width, HEAD_DIMENSION
    )
    pieces = (
        lax.all_gather(prompt_key_array, ("cand", "seq"), axis=0, tiled=True),
        lax.all_gather(prompt_value_array, ("cand", "seq"), axis=0, tiled=True),
    )
    key_pos = jnp.arange(pieces[0].shape[0], dtype=jnp.int32)

    def allowed_of(block_pos):
        return block_pos[None, None, :] < my_offsets[:, None, None]

    running = fold_blocks(
        (
            jnp.full(
                (candidate_local, KEY_VALUE_HEADS, group_width, output_rows),
                lowest_score_value,
                jnp.float32,
            ),
            jnp.zeros((candidate_local, KEY_VALUE_HEADS, group_width, output_rows), jnp.float32),
            jnp.zeros(
                (candidate_local, KEY_VALUE_HEADS, group_width, output_rows, HEAD_DIMENSION),
                jnp.float32,
            ),
        ),
        query_rows,
        pieces[0],
        pieces[1],
        key_pos,
        allowed_of,
        True,
    )
    pieces = (
        lax.all_gather(response_key_array, "seq", axis=1, tiled=True),
        lax.all_gather(response_value_array, "seq", axis=1, tiled=True),
    )
    key_pos = jnp.arange(pieces[0].shape[1], dtype=jnp.int32)

    def allowed_of(block_pos):
        causal = block_pos[None, None, :] <= query_pos[None, :, None]
        return causal & (block_pos[None, None, :] < my_lengths[:, None, None])

    final_max, final_total, final_sum = fold_blocks(
        running, query_rows, pieces[0], pieces[1], key_pos, allowed_of, False
    )
    attended = final_sum / final_total[..., None]
    attended = jnp.transpose(attended, (0, 3, 1, 2, 4)).reshape(candidate_local, output_rows, width)
    row_valid = query_pos[None, :] < my_lengths[:, None]
    attended = jnp.where(row_valid[:, :, None], attended, 0.0).astype(jnp.bfloat16)
    gathered = lax.all_gather(attended, "cand", axis=0, tiled=True)
    every_cand = jnp.arange(gathered.shape[0], dtype=jnp.int32)
    chosen = []
    for within in range(candidate_local):
        target = first_cand + within
        source = jnp.sum(jnp.where(ranks == target, every_cand, 0))
        chosen.append(lax.dynamic_index_in_dim(gathered, source, 0, keepdims=False))
    return jnp.stack(chosen, axis=0)


def solution(mesh):
    in_specs = (
        P("cand", "seq", None),
        P("cand", "seq", None),
        P("cand", "seq", None),
        P(("cand", "seq"), None),
        P(("cand", "seq"), None),
        P(),
        P(),
        P(),
    )
    out_specs = P("cand", "seq", None)
    return jax.shard_map(body, mesh=mesh, in_specs=in_specs, out_specs=out_specs, check_vma=False)
```

profile of v0, /device:TPU:0, one launch (start us, length us, event | category | flops | bytes accessed | tf_op | source)
XLA Modules:
  0.0 304.9 jit_solution(10088347945177968936)
XLA Ops:
  6.5 0.7 all-gather.6.cloned.1.call-update
  8.1 1.8 copy.56
  9.9 1.8 copy.57
  11.9 1.7 copy.52
  14.3 1.4 copy.62
  15.9 53.7 %all-gather.6.cloned.1.call-done = bf16[2048,512]{1,0:T(8,128)(2,1)} async-done(((bf16[64,512]{1,0:T(8,128)(2,1)}), bf16[2048,512]{1,0:T(8,128)(2,1)}) %all-gather.6.cloned.1.call-update) | async-done | bytes 2097168 | tf_op jit(solution)/shard_map/all_gather | solution.py:90
  69.6 58.4 %all-gather.8.cloned.1.call-done = bf16[2048,512]{1,0:T(8,128)(2,1)} async-done(((bf16[64,512]{1,0:T(8,128)(2,1)}), bf16[2048,512]{1,0:T(8,128)(2,1)}) %all-gather.8.cloned.1.call-update) | async-done | bytes 2097168 | tf_op jit(solution)/shard_map/all_gather | solution.py:91
  128.0 65.4 %while.37 = (s32[]{:T(128)}, f32[2,4,5,96]{3,2,0,1:T(8,128)S(1)}, f32[2,4,5,96]{3,2,0,1:T(8,128)S(1)}, f32[2,4,5,96,128]{4,3,2,0,1:T(8,128)}, s32[2048]{0:T(1024...) while((s32[]{:T(128)}, f32[2,4,5,96]{3,2,0,1:T(8,128)S(1)}, ...), condition=%wide.region_3.4_spmd.clone, body=%wide.region_0.3_spmd.clone.sunk | while | flops 1029754624 | bytes 34007236 | solution.py:65
  128.1 1.3 constant_dynamic-slice_fusion.9
  129.6 4.2 %fusion.60 = (f32[2,4,5,96]{3,2,0,1:T(8,128)S(1)}, f32[4,512,2,96,5]{1,3,4,2,0:T(8,128)}) fusion(pred[2,512]{1,0:T(4,128)(4,1)S(1)} %broadcast_compare_fusion.9, bf16[512,4,128,1,1]{0,2,4,3,1:T(8,128)(2,1)S(1)} %bitcast.88, bf16[2,96,4,5,128]{4,1,3,0,2:T(8,128)(2,1)S(1)} %get-tuple-element.683), kind=kOutput, calls=%fused_computation.26.clone.1 | convolution fusion | flops 509210880 | bytes 9388032 | tf_op jit(solution)/shard_map/while/body/eval_jaxpr/crhgd,nhd->chgrn/dot_general | solution.py:22
  133.9 4.5 %fusion.61 = f32[2,4,5,96]{3,2,0,1:T(8,128)S(1)} fusion(f32[4,512,2,96,5]{1,3,4,2,0:T(8,128)} %get-tuple-element.646, f32[2,4,5,96]{3,2,0,1:T(8,128)S(1)} %select_maximum_fusion.2, pred[2,512]{1,0:T(4,128)(4,1)S(1)} %broadcast_compare_fusion.9), kind=kLoop, calls=%fused_computation.25.clone.1 | loop fusion | flops 7860480 | bytes 7896064 | tf_op jit(solution)/shard_map/while/body/eval_jaxpr/reduce_sum | solution.py:36
  138.6 5.4 %bitcast_add_fusion.2 = f32[2,4,5,96,128]{4,3,2,0,1:T(8,128)} fusion(f32[2,4,5,96,128]{4,3,2,0,1:T(8,128)} %get-tuple-element.666, bf16[512,4,128,1,1]{0,2,4,3,1:T(8,128)(2,1)S(1)} %bitcast.91, f32[4,512,2,96,5]{1,3,4,2,0:T(8,128)} %get-tuple-element.646, f32[2,4,5,96]{3,2,0,1:T(8,128)S(1)} %select_maximum_fusion.2, ...), kind=kOutput, calls=%fused_computation.32.clone.1 | convolution fusion | flops 512655360 | bytes 12352513 | tf_op jit(solution)/shard_map/while/body/eval_jaxpr/chgrn,nhd->chgrd/dot_general | solution.py:38
  144.2 1.3 constant_dynamic-slice_fusion.9
  145.7 4.2 %fusion.60 = (f32[2,4,5,96]{3,2,0,1:T(8,128)S(1)}, f32[4,512,2,96,5]{1,3,4,2,0:T(8,128)}) fusion(pred[2,512]{1,0:T(4,128)(4,1)S(1)} %broadcast_compare_fusion.9, bf16[512,4,128,1,1]{0,2,4,3,1:T(8,128)(2,1)S(1)} %bitcast.88, bf16[2,96,4,5,128]{4,1,3,0,2:T(8,128)(2,1)S(1)} %get-tuple-element.683), kind=kOutput, calls=%fused_computation.26.clone.1 | convolution fusion | flops 509210880 | bytes 9388032 | tf_op jit(solution)/shard_map/while/body/eval_jaxpr/crhgd,nhd->chgrn/dot_general | solution.py:22
  149.9 4.4 %fusion.61 = f32[2,4,5,96]{3,2,0,1:T(8,128)S(1)} fusion(f32[4,512,2,96,5]{1,3,4,2,0:T(8,128)} %get-tuple-element.646, f32[2,4,5,96]{3,2,0,1:T(8,128)S(1)} %select_maximum_fusion.2, pred[2,512]{1,0:T(4,128)(4,1)S(1)} %broadcast_compare_fusion.9), kind=kLoop, calls=%fused_computation.25.clone.1 | loop fusion | flops 7860480 | bytes 7896064 | tf_op jit(solution)/shard_map/while/body/eval_jaxpr/reduce_sum | solution.py:36
  154.6 6.0 %bitcast_add_fusion.2 = f32[2,4,5,96,128]{4,3,2,0,1:T(8,128)} fusion(f32[2,4,5,96,128]{4,3,2,0,1:T(8,128)} %get-tuple-element.666, bf16[512,4,128,1,1]{0,2,4,3,1:T(8,128)(2,1)S(1)} %bitcast.91, f32[4,512,2,96,5]{1,3,4,2,0:T(8,128)} %get-tuple-element.646, f32[2,4,5,96]{3,2,0,1:T(8,128)S(1)} %select_maximum_fusion.2, ...), kind=kOutput, calls=%fused_computation.32.clone.1 | convolution fusion | flops 512655360 | bytes 12352513 | tf_op jit(solution)/shard_map/while/body/eval_jaxpr/chgrn,nhd->chgrd/dot_general | solution.py:38
  160.7 1.3 constant_dynamic-slice_fusion.9
  162.2 4.2 %fusion.60 = (f32[2,4,5,96]{3,2,0,1:T(8,128)S(1)}, f32[4,512,2,96,5]{1,3,4,2,0:T(8,128)}) fusion(pred[2,512]{1,0:T(4,128)(4,1)S(1)} %broadcast_compare_fusion.9, bf16[512,4,128,1,1]{0,2,4,3,1:T(8,128)(2,1)S(1)} %bitcast.88, bf16[2,96,4,5,128]{4,1,3,0,2:T(8,128)(2,1)S(1)} %get-tuple-element.683), kind=kOutput, calls=%fused_computation.26.clone.1 | convolution fusion | flops 509210880 | bytes 9388032 | tf_op jit(solution)/shard_map/while/body/eval_jaxpr/crhgd,nhd->chgrn/dot_general | solution.py:22
  166.4 4.4 %fusion.61 = f32[2,4,5,96]{3,2,0,1:T(8,128)S(1)} fusion(f32[4,512,2,96,5]{1,3,4,2,0:T(8,128)} %get-tuple-element.646, f32[2,4,5,96]{3,2,0,1:T(8,128)S(1)} %select_maximum_fusion.2, pred[2,512]{1,0:T(4,128)(4,1)S(1)} %broadcast_compare_fusion.9), kind=kLoop, calls=%fused_computation.25.clone.1 | loop fusion | flops 7860480 | bytes 7896064 | tf_op jit(solution)/shard_map/while/body/eval_jaxpr/reduce_sum | solution.py:36
  171.1 5.9 %bitcast_add_fusion.2 = f32[2,4,5,96,128]{4,3,2,0,1:T(8,128)} fusion(f32[2,4,5,96,128]{4,3,2,0,1:T(8,128)} %get-tuple-element.666, bf16[512,4,128,1,1]{0,2,4,3,1:T(8,128)(2,1)S(1)} %bitcast.91, f32[4,512,2,96,5]{1,3,4,2,0:T(8,128)} %get-tuple-element.646, f32[2,4,5,96]{3,2,0,1:T(8,128)S(1)} %select_maximum_fusion.2, ...), kind=kOutput, calls=%fused_computation.32.clone.1 | convolution fusion | flops 512655360 | bytes 12352513 | tf_op jit(solution)/shard_map/while/body/eval_jaxpr/chgrn,nhd->chgrd/dot_general | solution.py:38
  177.1 1.3 constant_dynamic-slice_fusion.9
  178.6 4.2 %fusion.60 = (f32[2,4,5,96]{3,2,0,1:T(8,128)S(1)}, f32[4,512,2,96,5]{1,3,4,2,0:T(8,128)}) fusion(pred[2,512]{1,0:T(4,128)(4,1)S(1)} %broadcast_compare_fusion.9, bf16[512,4,128,1,1]{0,2,4,3,1:T(8,128)(2,1)S(1)} %bitcast.88, bf16[2,96,4,5,128]{4,1,3,0,2:T(8,128)(2,1)S(1)} %get-tuple-element.683), kind=kOutput, calls=%fused_computation.26.clone.1 | convolution fusion | flops 509210880 | bytes 9388032 | tf_op jit(solution)/shard_map/while/body/eval_jaxpr/crhgd,nhd->chgrn/dot_general | solution.py:22
  182.8 4.4 %fusion.61 = f32[2,4,5,96]{3,2,0,1:T(8,128)S(1)} fusion(f32[4,512,2,96,5]{1,3,4,2,0:T(8,128)} %get-tuple-element.646, f32[2,4,5,96]{3,2,0,1:T(8,128)S(1)} %select_maximum_fusion.2, pred[2,512]{1,0:T(4,128)(4,1)S(1)} %broadcast_compare_fusion.9), kind=kLoop, calls=%fused_computation.25.clone.1 | loop fusion | flops 7860480 | bytes 7896064 | tf_op jit(solution)/shard_map/while/body/eval_jaxpr/reduce_sum | solution.py:36
  187.5 5.9 %bitcast_add_fusion.2 = f32[2,4,5,96,128]{4,3,2,0,1:T(8,128)} fusion(f32[2,4,5,96,128]{4,3,2,0,1:T(8,128)} %get-tuple-element.666, bf16[512,4,128,1,1]{0,2,4,3,1:T(8,128)(2,1)S(1)} %bitcast.91, f32[4,512,2,96,5]{1,3,4,2,0:T(8,128)} %get-tuple-element.646, f32[2,4,5,96]{3,2,0,1:T(8,128)S(1)} %select_maximum_fusion.2, ...), kind=kOutput, calls=%fused_computation.32.clone.1 | convolution fusion | flops 512655360 | bytes 12352513 | tf_op jit(solution)/shard_map/while/body/eval_jaxpr/chgrn,nhd->chgrd/dot_general | solution.py:38
  193.4 1.7 copy.60
  196.3 22.1 %all-gather.12.cloned.1.call-done = bf16[2,768,512]{2,0,1:T(2,128)(2,1)} async-done(((bf16[2,96,512]{2,0,1:T(2,128)(2,1)}), bf16[2,768,512]{2,0,1:T(2,128)(2,1)}) %all-gather.12.cloned.1.call-update) | async-done | bytes 1572880 | tf_op jit(solution)/shard_map/all_gather | solution.py:120
  218.4 41.8 %while.36 = (s32[]{:T(128)}, f32[2,4,5,96]{3,2,1,0:T(8,128)}, f32[2,4,5,96]{3,2,1,0:T(8,128)}, f32[2,4,5,96,128]{4,3,2,1,0:T(8,128)S(1)}, s32[768]{0:T(1024)S(1)...) while((s32[]{:T(128)}, f32[2,4,5,96]{3,2,1,0:T(8,128)}, ...), condition=%wide.region_7.8_spmd.clone, body=%wide.region_4.7_spmd.clone.sunk | while | flops 515194976 | bytes 38561872 | solution.py:65
  219.3 1.9 constant_dynamic-slice_fusion.8
  221.8 2.2 fusion.54
  224.0 1.8 copy-done
  225.9 1.5 fusion.55
  228.0 3.7 %multiply_add_fusion.5 = f32[2,4,5,96,128]{4,3,2,1,0:T(8,128)S(1)} fusion(f32[2,4,5,96,128]{4,3,2,1,0:T(8,128)S(1)} %get-tuple-element.706, bf16[2,256,4,128,1]{1,3,4,2,0:T(8,128)(2,1)S(1)} %bitcast.89, f32[2,4,256,96,5]{2,3,4,1,0:T(8,128)} %copy-done, f32[2,4,5,96]{3,2,1,0:T(8,128)S(1)} %max.19, pred[2,96,256]{2,1,0:T(8,128)(4,1)S(1)} %copy-done.1, ...), kind=kOutput, calls=%fused_computation.7.clone.1 | convolution fusion | flops 256573440 | bytes 8468480 | tf_op jit(solution)/shard_map/while/body/eval_jaxpr/chgrn,cnhd->chgrd/dot_general | solution.py:42
  233.2 1.9 constant_dynamic-slice_fusion.8
  235.7 2.2 fusion.54
  238.0 1.8 copy-done
  239.8 1.5 fusion.55
  241.9 3.7 %multiply_add_fusion.5 = f32[2,4,5,96,128]{4,3,2,1,0:T(8,128)S(1)} fusion(f32[2,4,5,96,128]{4,3,2,1,0:T(8,128)S(1)} %get-tuple-element.706, bf16[2,256,4,128,1]{1,3,4,2,0:T(8,128)(2,1)S(1)} %bitcast.89, f32[2,4,256,96,5]{2,3,4,1,0:T(8,128)} %copy-done, f32[2,4,5,96]{3,2,1,0:T(8,128)S(1)} %max.19, pred[2,96,256]{2,1,0:T(8,128)(4,1)S(1)} %copy-done.1, ...), kind=kOutput, calls=%fused_computation.7.clone.1 | convolution fusion | flops 256573440 | bytes 8468480 | tf_op jit(solution)/shard_map/while/body/eval_jaxpr/chgrn,cnhd->chgrd/dot_general | solution.py:42
  247.2 1.9 constant_dynamic-slice_fusion.8
  249.7 2.2 fusion.54
  251.9 1.8 copy-done
  253.7 1.5 fusion.55
  255.9 3.7 %multiply_add_fusion.5 = f32[2,4,5,96,128]{4,3,2,1,0:T(8,128)S(1)} fusion(f32[2,4,5,96,128]{4,3,2,1,0:T(8,128)S(1)} %get-tuple-element.706, bf16[2,256,4,128,1]{1,3,4,2,0:T(8,128)(2,1)S(1)} %bitcast.89, f32[2,4,256,96,5]{2,3,4,1,0:T(8,128)} %copy-done, f32[2,4,5,96]{3,2,1,0:T(8,128)S(1)} %max.19, pred[2,96,256]{2,1,0:T(8,128)(4,1)S(1)} %copy-done.1, ...), kind=kOutput, calls=%fused_computation.7.clone.1 | convolution fusion | flops 256573440 | bytes 8468480 | tf_op jit(solution)/shard_map/while/body/eval_jaxpr/chgrn,cnhd->chgrd/dot_general | solution.py:42
  260.2 1.3 divide_bitcast_fusion
  261.5 0.8 copy.64
  262.9 1.2 select_convert_fusion
  268.5 27.6 %all-gather.14.cloned.1.call-done = bf16[8,96,2560]{2,1,0:T(8,128)(2,1)} async-done(((bf16[2,96,2560]{2,1,0:T(8,128)(2,1)}), bf16[8,96,2560]{2,1,0:T(8,128)(2,1)}) %all-gather.14.cloned.1.call-update) | async-done | bytes 3932176 | tf_op jit(solution)/shard_map/all_gather | solution.py:135
  296.1 1.2 constant_dynamic-slice_fusion.5
  297.3 1.0 pad_maximum_fusion
  (115 shorter events, 14.7 us)
Async XLA Ops:
  6.5 63.1 %all-gather.6.cloned.1.call-start = ((), (), s32[]{:S(2)}) async-start(), calls=%async_computation | async-start | bytes 2162688 | tf_op jit(solution)/shard_map/all_gather | solution.py:90
  7.3 120.7 %all-gather.8.cloned.1.call-start = ((), (), s32[]{:S(2)}) async-start(), calls=%async_computation.1 | async-start | bytes 2162688 | tf_op jit(solution)/shard_map/all_gather | solution.py:91
  8.0 188.3 %all-gather.10.cloned.1.call-start = ((), (), s32[]{:S(2)}) async-start(), calls=%async_computation.2 | async-start | bytes 1769472 | tf_op jit(solution)/shard_map/all_gather | solution.py:119
  9.9 5.8 %copy-start.6 = (s32[8]{0:T(128)S(1)}, s32[8]{0:T(128)}, u32[]{:S(2)}) copy-start(s32[8]{0:T(128)} %param.18) | copy-start | bytes 100
  9.9 5.9 %copy-start.7 = (s32[8]{0:T(128)S(1)}, s32[8]{0:T(128)}, u32[]{:S(2)}) copy-start(s32[8]{0:T(128)} %param.17) | copy-start | bytes 100
  9.9 208.5 %all-gather.12.cloned.1.call-start = ((), (), s32[]{:S(2)}) async-start(), calls=%async_computation.3 | async-start | bytes 1769472 | tf_op jit(solution)/shard_map/all_gather | solution.py:120
  11.8 284.3 %all-gather.14.cloned.1.call-start = ((), (), s32[]{:S(2)}) async-start(), calls=%async_computation.4 | async-start | bytes 4915200 | tf_op jit(solution)/shard_map/all_gather | solution.py:135
  221.8 2.2 copy-start.2
  221.8 4.1 %copy-start.1 = (pred[2,96,256]{2,1,0:T(8,128)(4,1)S(1)}, pred[2,96,256]{2,1,0:T(8,128)(4,1)}, u32[]{:S(2)}) copy-start(pred[2,96,256]{2,1,0:T(8,128)(4,1)} %broadcast_and_fusion.2) | copy-start | bytes 147460 | tf_op jit(solution)/shard_map/while
  221.8 5.6 %copy-start.3 = (f32[2,4,5,96]{3,2,1,0:T(8,128)S(1)}, f32[2,4,5,96]{3,2,1,0:T(8,128)}, u32[]{:S(2)}) copy-start(f32[2,4,5,96]{3,2,1,0:T(8,128)} %get-tuple-element.705) | copy-start | bytes 46084 | tf_op jit(solution)/shard_map/while
  224.0 1.8 copy-start
  227.4 4.3 %copy-start.4 = (f32[2,4,5,96]{3,2,1,0:T(8,128)}, f32[2,4,5,96]{3,2,1,0:T(8,128)S(1)}, u32[]{:S(2)}) copy-start(f32[2,4,5,96]{3,2,1,0:T(8,128)S(1)} %get-tuple-element.719) | copy-start | bytes 46084 | tf_op jit(solution)/shard_map/while
  235.7 2.2 copy-start.2
  235.7 4.1 %copy-start.1 = (pred[2,96,256]{2,1,0:T(8,128)(4,1)S(1)}, pred[2,96,256]{2,1,0:T(8,128)(4,1)}, u32[]{:S(2)}) copy-start(pred[2,96,256]{2,1,0:T(8,128)(4,1)} %broadcast_and_fusion.2) | copy-start | bytes 147460 | tf_op jit(solution)/shard_map/while
  235.7 5.6 %copy-start.3 = (f32[2,4,5,96]{3,2,1,0:T(8,128)S(1)}, f32[2,4,5,96]{3,2,1,0:T(8,128)}, u32[]{:S(2)}) copy-start(f32[2,4,5,96]{3,2,1,0:T(8,128)} %get-tuple-element.705) | copy-start | bytes 46084 | tf_op jit(solution)/shard_map/while
  237.9 1.8 copy-start
  241.4 4.3 %copy-start.4 = (f32[2,4,5,96]{3,2,1,0:T(8,128)}, f32[2,4,5,96]{3,2,1,0:T(8,128)S(1)}, u32[]{:S(2)}) copy-start(f32[2,4,5,96]{3,2,1,0:T(8,128)S(1)} %get-tuple-element.719) | copy-start | bytes 46084 | tf_op jit(solution)/shard_map/while
  249.6 2.2 copy-start.2
  249.6 4.1 %copy-start.1 = (pred[2,96,256]{2,1,0:T(8,128)(4,1)S(1)}, pred[2,96,256]{2,1,0:T(8,128)(4,1)}, u32[]{:S(2)}) copy-start(pred[2,96,256]{2,1,0:T(8,128)(4,1)} %broadcast_and_fusion.2) | copy-start | bytes 147460 | tf_op jit(solution)/shard_map/while
  249.7 5.6 %copy-start.3 = (f32[2,4,5,96]{3,2,1,0:T(8,128)S(1)}, f32[2,4,5,96]{3,2,1,0:T(8,128)}, u32[]{:S(2)}) copy-start(f32[2,4,5,96]{3,2,1,0:T(8,128)} %get-tuple-element.705) | copy-start | bytes 46084 | tf_op jit(solution)/shard_map/while
  251.9 1.8 copy-start
  255.3 4.3 %copy-start.4 = (f32[2,4,5,96]{3,2,1,0:T(8,128)}, f32[2,4,5,96]{3,2,1,0:T(8,128)S(1)}, u32[]{:S(2)}) copy-start(f32[2,4,5,96]{3,2,1,0:T(8,128)S(1)} %get-tuple-element.719) | copy-start | bytes 46084 | tf_op jit(solution)/shard_map/while
  261.5 2.6 copy-start.5
Sparse Core Ops, SparseCore 0:
  10.3 59.2 all-gather.5
  72.6 55.3 all-gather.7
  130.2 43.0 all-gather.9
  175.3 43.0 all-gather.11
  264.3 31.7 all-gather.13
where the time goes:
time: 306 us; the launch traced here: 305 us
  waiting for transfers between devices  163 us (53%)
  matrix products  57.7 us (19%)
  local copies, waits for them, and re-layouts  36.7 us (12%)
  other arithmetic  29.6 us (10%)
  between operations  16.9 us (6%)
    all_gather x1, waiting for transfers between devices, body(): lax.all_gather(prompt_value_array, ('cand', 'seq'), axis=0, tiled=True)  58.4 us
    all_gather x1, waiting for transfers between devices, body(): lax.all_gather(prompt_key_array, ('cand', 'seq'), axis=0, tiled=True)  53.7 us
    all_gather x1, waiting for transfers between devices, body(): gathered = lax.all_gather(attended, 'cand', axis=0, tiled=True)  27.6 us
    dot_general x4, matrix products, attend_block(): jnp.einsum('chgrn,nhd->chgrd', weights, values_split, preferred_element_t...  23.1 us
    reduce_sum x7, other arithmetic, attend_block(): new_total = running_total * rescale + jnp.sum(exponent, axis=-1)  22.3 us
    all_gather x1, waiting for transfers between devices, body(): lax.all_gather(response_value_array, 'seq', axis=1, tiled=True)  22.1 us
    dot_general x4, matrix products, attend_block(): jnp.einsum('crhgd,nhd->chgrn', query_rows, keys_split, preferred_element_...  16.9 us
    dynamic_slice x14, local copies, waits for them, and re-layouts, one_block(): lax.dynamic_slice_in_dim(all_values, block_start, block_len, keys_axis)  13.3 us
  transfers between devices with their start and end apart: 5, of which 4 were waited for; matrix products, arithmetic and copies ran while one was open for 25% of the time, Pallas kernels for 0%

commit v1 on v0

--- a/solution.py
+++ b/solution.py
@@ -86,9 +86,25 @@
     query_rows = response_query_array.reshape(
         candidate_local, output_rows, KEY_VALUE_HEADS, group_width, HEAD_DIMENSION
     )
+
+    def drive_vector_now(u, named_axis):
+        piece_next, extra, long_array = (
+            lax.axis_size(named_axis),
+            lax.axis_index(named_axis),
+            u.shape[0],
+        )
+        lower, v_next = (u, 1)
+        while v_next < piece_next:
+            all_rows = []
+            for k in tuple(range(piece_next)):
+                all_rows.append((k, (k - v_next) % piece_next))
+            lower = jnp.concatenate([lower, lax.ppermute(lower, named_axis, all_rows)], 0)
+            v_next = 2 * v_next
+        return jnp.roll(lower, extra * long_array, 0)
+
     pieces = (
         lax.all_gather(prompt_key_array, ("cand", "seq"), axis=0, tiled=True),
-        lax.all_gather(prompt_value_array, ("cand", "seq"), axis=0, tiled=True),
+        drive_vector_now(prompt_value_array, ("cand", "seq")),
     )
     key_pos = jnp.arange(pieces[0].shape[0], dtype=jnp.int32)
 

time: 306 us -> 256 us (0.84)
  waiting for transfers between devices: 163 us -> 91.6 us
  local copies, waits for them, and re-layouts: 36.7 us -> 52.4 us
  starting transfers between devices: 0.16 us -> 8.75 us
  matrix products: 57.7 us -> 53.5 us
    all_gather x1 -> x0, waiting for transfers between devices: 58.4 us -> none  [body(): lax.all_gather(prompt_value_array, ('cand', 'seq'), axis=0, tiled=True)]
    ppermute x0 -> x5, waiting for transfers between devices: none -> 54.7 us  [drive_vector_now(): lax.ppermute(lower, named_axis, all_rows)]
    all_gather x1, waiting for transfers between devices: 53.7 us -> 0.01 us  [body(): lax.all_gather(prompt_key_array, ('cand', 'seq'), axis=0, tiled=True)]
    all_gather x1, waiting for transfers between devices: 22.1 us -> 8.61 us  [body(): lax.all_gather(response_value_array, 'seq', axis=1, tiled=True)]
    concatenate x0 -> x2, local copies, waits for them, and re-layouts: none -> 9.46 us  [the longest x1 7.51 us: drive_vector_now(): return jnp.roll(lower, extra * long_array, 0)]
    ppermute x0 -> x5, starting transfers between devices: none -> 8.63 us  [drive_vector_now(): lax.ppermute(lower, named_axis, all_rows)]
    dynamic_slice x7 -> x11, local copies, waits for them, and re-layouts: 2.48 us -> 6.79 us  [one_block(): lax.dynamic_slice_in_dim(all_keys, block_start, block_len, keys_axis)]
    dot_general x4, matrix products: 23.1 us -> 18.9 us  [attend_block(): jnp.einsum('chgrn,nhd->chgrd', weights, values_split, preferred_element_t...]
  transfers between devices with their start and end apart: 5 -> 9, of which waited for: 4 -> 7; matrix products, arithmetic and copies ran while one was open for 25% -> 35% of each run, Pallas kernels for 0% -> 0%
where the time goes in v1:
time: 256 us; the launch traced here: 254 us
  waiting for transfers between devices  91.6 us (36%)
  matrix products  53.5 us (21%)
  local copies, waits for them, and re-layouts  52.4 us (20%)
  other arithmetic  30.5 us (12%)
  between operations  17 us (7%)
  starting transfers between devices  8.75 us (3%)
    ppermute x5, waiting for transfers between devices, drive_vector_now(): lax.ppermute(lower, named_axis, all_rows)  54.7 us
    all_gather x1, waiting for transfers between devices, body(): gathered = lax.all_gather(attended, 'cand', axis=0, tiled=True)  27.5 us
    reduce_sum x7, other arithmetic, attend_block(): new_total = running_total * rescale + jnp.sum(exponent, axis=-1)  22.9 us
    dot_general x4, matrix products, attend_block(): jnp.einsum('chgrn,nhd->chgrd', weights, values_split, preferred_element_t...  18.9 us
    dot_general x4, matrix products, attend_block(): jnp.einsum('crhgd,nhd->chgrn', query_rows, keys_split, preferred_element_...  16.9 us
    dynamic_slice x10, local copies, waits for them, and re-layouts, one_block(): lax.dynamic_slice_in_dim(all_values, block_start, block_len, keys_axis)  11.9 us
    dot_general x3, matrix products, attend_block(): jnp.einsum('chgrn,cnhd->chgrd', weights, values_split, preferred_element_...  11.1 us
    unnamed x19, local copies, waits for them, and re-layouts  9.41 us
  transfers between devices with their start and end apart: 9, of which 7 were waited for; matrix products, arithmetic and copies ran while one was open for 35% of the time, Pallas kernels for 0%

profile of v1, /device:TPU:0, one launch (start us, length us, event | category | flops | bytes accessed | tf_op | source)
XLA Modules:
  0.0 254.4 jit_solution(15693656871667753655)
XLA Ops:
  7.3 1.8 copy.74
  10.1 6.4 %collective-permute-start = (bf16[64,512]{0,1:T(8,128)(2,1)S(1)}, bf16[64,512]{0,1:T(8,128)(2,1)S(1)}, u32[]{:S(2)}, u32[]{:S(2)}) collective-permute-start(bf16[64,512]{0,1:T(8,128)(2,1)S(1)} %copy.70), channel_id=1, source_target_pairs={{0,31},{1,0},{2,1},{3,2},{4,3},{5,4},{6,5},{7,6},{8,7},{9,8},{10,9... | collective-permute-start | bytes 196616 | tf_op jit(solution)/shard_map/ppermute | solution.py:101
  16.6 2.9 %collective-permute-done = bf16[64,512]{0,1:T(8,128)(2,1)S(1)} collective-permute-done((bf16[64,512]{0,1:T(8,128)(2,1)S(1)}, bf16[64,512]{0,1:T(8,128)(2,1)S(1)}, u32[]{:S(2)}, u32[]{:S(2)}) %collective-permute-start) | collective-permute-done | bytes 65568 | tf_op jit(solution)/shard_map/ppermute | solution.py:101
  20.2 4.6 %collective-permute-done.1 = bf16[128,512]{0,1:T(8,128)(2,1)S(1)} collective-permute-done((bf16[128,512]{0,1:T(8,128)(2,1)S(1)}, bf16[128,512]{0,1:T(8,128)(2,1)S(1)}, u32[]{:S(2)}, u32[]{:S(2)}) %collective-permute-start.1) | collective-permute-done | bytes 131104 | tf_op jit(solution)/shard_map/ppermute | solution.py:101
  24.9 15.4 %collective-permute-done.2 = bf16[256,512]{0,1:T(8,128)(2,1)S(1)} collective-permute-done((bf16[256,512]{0,1:T(8,128)(2,1)S(1)}, bf16[256,512]{0,1:T(8,128)(2,1)S(1)}, u32[]{:S(2)}, u32[]{:S(2)}) %collective-permute-start.2) | collective-permute-done | bytes 262176 | tf_op jit(solution)/shard_map/ppermute | solution.py:101
  40.6 8.5 %collective-permute-done.3 = bf16[512,512]{0,1:T(8,128)(2,1)S(1)} collective-permute-done((bf16[512,512]{0,1:T(8,128)(2,1)S(1)}, bf16[512,512]{0,1:T(8,128)(2,1)S(1)}, u32[]{:S(2)}, u32[]{:S(2)}) %collective-permute-start.3) | collective-permute-done | bytes 524320 | tf_op jit(solution)/shard_map/ppermute | solution.py:101
  49.1 1.9 concatenate.25
  51.1 1.5 collective-permute-start.4
  55.0 1.4 copy.80
  56.6 23.3 %collective-permute-done.4 = bf16[1024,512]{0,1:T(8,128)(2,1)} collective-permute-done((bf16[1024,512]{0,1:T(8,128)(2,1)}, bf16[1024,512]{0,1:T(8,128)(2,1)}, u32[]{:S(2)}, u32[]{:S(2)}) %collective-permute-start.4) | collective-permute-done | bytes 1048608 | tf_op jit(solution)/shard_map/ppermute | solution.py:101
  79.9 7.5 %concatenate.26 = bf16[4096,512]{0,1:T(8,128)(2,1)} concatenate(bf16[64,512]{0,1:T(8,128)(2,1)S(1)} %copy.70, bf16[64,512]{0,1:T(8,128)(2,1)S(1)} %collective-permute-done, bf16[128,512]{0,1:T(8,128)(2,1)S(1)} %collective-permute-done.1, bf16[256,512]{0,1:T(8,128)(2,1)S(1)} %collective-permute-done.2, bf16[512,512]{0,1:T(8,128)(2,1)S(1)} %collective-permute-done.3, ...), dimensions={0} | concatenate | bytes 8388608 | tf_op jit(solution)/shard_map/jit(_roll_dynamic)/concatenate | solution.py:103
  87.4 4.2 %constant_dynamic-slice_fusion.6 = bf16[2048,512]{0,1:T(8,128)(2,1)} fusion(bf16[4096,512]{0,1:T(8,128)(2,1)} %concatenate.26, s32[]{:T(128)S(6)} %select_n.71), kind=kLoop, calls=%fused_computation.53 | loop fusion | bytes 4194308 | tf_op jit(solution)/shard_map/jit(_roll_dynamic)/dynamic_slice | solution.py:103
  91.6 64.7 %while.37 = (s32[]{:T(128)}, f32[2,4,5,96]{3,2,0,1:T(8,128)S(1)}, f32[2,4,5,96]{3,2,0,1:T(8,128)S(1)}, f32[2,4,5,96,128]{4,3,2,0,1:T(8,128)}, s32[2048]{0:T(1024...) while((s32[]{:T(128)}, f32[2,4,5,96]{3,2,0,1:T(8,128)S(1)}, ...), condition=%wide.region_3.4_spmd.clone, body=%wide.region_0.3_spmd.clone.sunk | while | flops 1029754624 | bytes 64415972 | solution.py:65
  93.1 4.2 %fusion.60 = (f32[2,4,5,96]{3,2,0,1:T(8,128)S(1)}, f32[4,512,2,96,5]{1,3,4,2,0:T(8,128)}) fusion(pred[2,512]{1,0:T(4,128)(4,1)S(1)} %broadcast_compare_fusion.9, bf16[512,4,128,1,1]{0,2,4,3,1:T(8,128)(2,1)S(1)} %bitcast.88, bf16[2,96,4,5,128]{4,1,3,0,2:T(8,128)(2,1)S(1)} %get-tuple-element.677), kind=kOutput, calls=%fused_computation.26.clone.1 | convolution fusion | flops 509210880 | bytes 9388032 | tf_op jit(solution)/shard_map/while/body/eval_jaxpr/crhgd,nhd->chgrn/dot_general | solution.py:22
  97.3 4.5 %fusion.61 = f32[2,4,5,96]{3,2,0,1:T(8,128)S(1)} fusion(f32[4,512,2,96,5]{1,3,4,2,0:T(8,128)} %get-tuple-element.641, f32[2,4,5,96]{3,2,0,1:T(8,128)S(1)} %select_maximum_fusion.2, pred[2,512]{1,0:T(4,128)(4,1)S(1)} %broadcast_compare_fusion.9), kind=kLoop, calls=%fused_computation.25.clone.1 | loop fusion | flops 7860480 | bytes 7896064 | tf_op jit(solution)/shard_map/while/body/eval_jaxpr/reduce_sum | solution.py:36
  102.9 3.7 %bitcast_add_fusion.2 = f32[2,4,5,96,128]{4,3,2,0,1:T(8,128)} fusion(f32[2,4,5,96,128]{4,3,2,0,1:T(8,128)} %get-tuple-element.660, bf16[512,4,128,1,1]{0,2,4,3,1:T(8,128)(2,1)S(1)} %bitcast.91, f32[4,512,2,96,5]{1,3,4,2,0:T(8,128)S(1)} %copy-done, f32[2,4,5,96]{3,2,0,1:T(8,128)S(1)} %select_maximum_fusion.2, ...), kind=kOutput, calls=%fused_computation.32.clone.1 | convolution fusion | flops 512655360 | bytes 12352513 | tf_op jit(solution)/shard_map/while/body/eval_jaxpr/chgrn,nhd->chgrd/dot_general | solution.py:38
  108.0 4.2 %fusion.60 = (f32[2,4,5,96]{3,2,0,1:T(8,128)S(1)}, f32[4,512,2,96,5]{1,3,4,2,0:T(8,128)}) fusion(pred[2,512]{1,0:T(4,128)(4,1)S(1)} %broadcast_compare_fusion.9, bf16[512,4,128,1,1]{0,2,4,3,1:T(8,128)(2,1)S(1)} %bitcast.88, bf16[2,96,4,5,128]{4,1,3,0,2:T(8,128)(2,1)S(1)} %get-tuple-element.677), kind=kOutput, calls=%fused_computation.26.clone.1 | convolution fusion | flops 509210880 | bytes 9388032 | tf_op jit(solution)/shard_map/while/body/eval_jaxpr/crhgd,nhd->chgrn/dot_general | solution.py:22
  112.3 4.5 %fusion.61 = f32[2,4,5,96]{3,2,0,1:T(8,128)S(1)} fusion(f32[4,512,2,96,5]{1,3,4,2,0:T(8,128)} %get-tuple-element.641, f32[2,4,5,96]{3,2,0,1:T(8,128)S(1)} %select_maximum_fusion.2, pred[2,512]{1,0:T(4,128)(4,1)S(1)} %broadcast_compare_fusion.9), kind=kLoop, calls=%fused_computation.25.clone.1 | loop fusion | flops 7860480 | bytes 7896064 | tf_op jit(solution)/shard_map/while/body/eval_jaxpr/reduce_sum | solution.py:36
  118.0 5.1 %bitcast_add_fusion.2 = f32[2,4,5,96,128]{4,3,2,0,1:T(8,128)} fusion(f32[2,4,5,96,128]{4,3,2,0,1:T(8,128)} %get-tuple-element.660, bf16[512,4,128,1,1]{0,2,4,3,1:T(8,128)(2,1)S(1)} %bitcast.91, f32[4,512,2,96,5]{1,3,4,2,0:T(8,128)S(1)} %copy-done, f32[2,4,5,96]{3,2,0,1:T(8,128)S(1)} %select_maximum_fusion.2, ...), kind=kOutput, calls=%fused_computation.32.clone.1 | convolution fusion | flops 512655360 | bytes 12352513 | tf_op jit(solution)/shard_map/while/body/eval_jaxpr/chgrn,nhd->chgrd/dot_general | solution.py:38
  124.5 4.2 %fusion.60 = (f32[2,4,5,96]{3,2,0,1:T(8,128)S(1)}, f32[4,512,2,96,5]{1,3,4,2,0:T(8,128)}) fusion(pred[2,512]{1,0:T(4,128)(4,1)S(1)} %broadcast_compare_fusion.9, bf16[512,4,128,1,1]{0,2,4,3,1:T(8,128)(2,1)S(1)} %bitcast.88, bf16[2,96,4,5,128]{4,1,3,0,2:T(8,128)(2,1)S(1)} %get-tuple-element.677), kind=kOutput, calls=%fused_computation.26.clone.1 | convolution fusion | flops 509210880 | bytes 9388032 | tf_op jit(solution)/shard_map/while/body/eval_jaxpr/crhgd,nhd->chgrn/dot_general | solution.py:22
  128.8 4.7 %fusion.61 = f32[2,4,5,96]{3,2,0,1:T(8,128)S(1)} fusion(f32[4,512,2,96,5]{1,3,4,2,0:T(8,128)} %get-tuple-element.641, f32[2,4,5,96]{3,2,0,1:T(8,128)S(1)} %select_maximum_fusion.2, pred[2,512]{1,0:T(4,128)(4,1)S(1)} %broadcast_compare_fusion.9), kind=kLoop, calls=%fused_computation.25.clone.1 | loop fusion | flops 7860480 | bytes 7896064 | tf_op jit(solution)/shard_map/while/body/eval_jaxpr/reduce_sum | solution.py:36
  134.6 5.1 %bitcast_add_fusion.2 = f32[2,4,5,96,128]{4,3,2,0,1:T(8,128)} fusion(f32[2,4,5,96,128]{4,3,2,0,1:T(8,128)} %get-tuple-element.660, bf16[512,4,128,1,1]{0,2,4,3,1:T(8,128)(2,1)S(1)} %bitcast.91, f32[4,512,2,96,5]{1,3,4,2,0:T(8,128)S(1)} %copy-done, f32[2,4,5,96]{3,2,0,1:T(8,128)S(1)} %select_maximum_fusion.2, ...), kind=kOutput, calls=%fused_computation.32.clone.1 | convolution fusion | flops 512655360 | bytes 12352513 | tf_op jit(solution)/shard_map/while/body/eval_jaxpr/chgrn,nhd->chgrd/dot_general | solution.py:38
  141.1 4.2 %fusion.60 = (f32[2,4,5,96]{3,2,0,1:T(8,128)S(1)}, f32[4,512,2,96,5]{1,3,4,2,0:T(8,128)}) fusion(pred[2,512]{1,0:T(4,128)(4,1)S(1)} %broadcast_compare_fusion.9, bf16[512,4,128,1,1]{0,2,4,3,1:T(8,128)(2,1)S(1)} %bitcast.88, bf16[2,96,4,5,128]{4,1,3,0,2:T(8,128)(2,1)S(1)} %get-tuple-element.677), kind=kOutput, calls=%fused_computation.26.clone.1 | convolution fusion | flops 509210880 | bytes 9388032 | tf_op jit(solution)/shard_map/while/body/eval_jaxpr/crhgd,nhd->chgrn/dot_general | solution.py:22
  145.4 4.5 %fusion.61 = f32[2,4,5,96]{3,2,0,1:T(8,128)S(1)} fusion(f32[4,512,2,96,5]{1,3,4,2,0:T(8,128)} %get-tuple-element.641, f32[2,4,5,96]{3,2,0,1:T(8,128)S(1)} %select_maximum_fusion.2, pred[2,512]{1,0:T(4,128)(4,1)S(1)} %broadcast_compare_fusion.9), kind=kLoop, calls=%fused_computation.25.clone.1 | loop fusion | flops 7860480 | bytes 7896064 | tf_op jit(solution)/shard_map/while/body/eval_jaxpr/reduce_sum | solution.py:36
  149.9 1.2 constant_dynamic-slice_fusion.12
  151.2 5.1 %bitcast_add_fusion.2 = f32[2,4,5,96,128]{4,3,2,0,1:T(8,128)} fusion(f32[2,4,5,96,128]{4,3,2,0,1:T(8,128)} %get-tuple-element.660, bf16[512,4,128,1,1]{0,2,4,3,1:T(8,128)(2,1)S(1)} %bitcast.91, f32[4,512,2,96,5]{1,3,4,2,0:T(8,128)S(1)} %copy-done, f32[2,4,5,96]{3,2,0,1:T(8,128)S(1)} %select_maximum_fusion.2, ...), kind=kOutput, calls=%fused_computation.32.clone.1 | convolution fusion | flops 512655360 | bytes 12352513 | tf_op jit(solution)/shard_map/while/body/eval_jaxpr/chgrn,nhd->chgrd/dot_general | solution.py:38
  156.3 1.7 copy.78
  159.2 8.6 %all-gather.9.cloned.1.call-done = bf16[2,768,512]{2,0,1:T(2,128)(2,1)} async-done(((bf16[2,96,512]{2,0,1:T(2,128)(2,1)}), bf16[2,768,512]{2,0,1:T(2,128)(2,1)}) %all-gather.9.cloned.1.call-update) | async-done | bytes 1572880 | tf_op jit(solution)/shard_map/all_gather | solution.py:136
  167.9 41.8 %while.36 = (s32[]{:T(128)}, f32[2,4,5,96]{3,2,1,0:T(8,128)}, f32[2,4,5,96]{3,2,1,0:T(8,128)}, f32[2,4,5,96,128]{4,3,2,1,0:T(8,128)S(1)}, s32[768]{0:T(1024)S(1)...) while((s32[]{:T(128)}, f32[2,4,5,96]{3,2,1,0:T(8,128)}, ...), condition=%wide.region_7.8_spmd.clone, body=%wide.region_4.7_spmd.clone.sunk | while | flops 515194976 | bytes 38561872 | solution.py:65
  168.7 1.9 constant_dynamic-slice_fusion.10
  171.2 2.2 fusion.54
  173.5 1.8 copy-done.1
  175.3 1.5 fusion.55
  177.5 3.7 %multiply_add_fusion.5 = f32[2,4,5,96,128]{4,3,2,1,0:T(8,128)S(1)} fusion(f32[2,4,5,96,128]{4,3,2,1,0:T(8,128)S(1)} %get-tuple-element.700, bf16[2,256,4,128,1]{1,3,4,2,0:T(8,128)(2,1)S(1)} %bitcast.89, f32[2,4,256,96,5]{2,3,4,1,0:T(8,128)} %copy-done.1, f32[2,4,5,96]{3,2,1,0:T(8,128)S(1)} %max.19, pred[2,96,256]{2,1,0:T(8,128)(4,1)S(1)} %copy-done.2, ...), kind=kOutput, calls=%fused_computation.7.clone.1 | convolution fusion | flops 256573440 | bytes 8468480 | tf_op jit(solution)/shard_map/while/body/eval_jaxpr/chgrn,cnhd->chgrd/dot_general | solution.py:42
  182.7 1.9 constant_dynamic-slice_fusion.10
  185.2 2.2 fusion.54
  187.4 1.8 copy-done.1
  189.3 1.5 fusion.55
  191.4 3.7 %multiply_add_fusion.5 = f32[2,4,5,96,128]{4,3,2,1,0:T(8,128)S(1)} fusion(f32[2,4,5,96,128]{4,3,2,1,0:T(8,128)S(1)} %get-tuple-element.700, bf16[2,256,4,128,1]{1,3,4,2,0:T(8,128)(2,1)S(1)} %bitcast.89, f32[2,4,256,96,5]{2,3,4,1,0:T(8,128)} %copy-done.1, f32[2,4,5,96]{3,2,1,0:T(8,128)S(1)} %max.19, pred[2,96,256]{2,1,0:T(8,128)(4,1)S(1)} %copy-done.2, ...), kind=kOutput, calls=%fused_computation.7.clone.1 | convolution fusion | flops 256573440 | bytes 8468480 | tf_op jit(solution)/shard_map/while/body/eval_jaxpr/chgrn,cnhd->chgrd/dot_general | solution.py:42
  196.6 1.9 constant_dynamic-slice_fusion.10
  199.1 2.2 fusion.54
  201.4 1.8 copy-done.1
  203.2 1.5 fusion.55
  205.3 3.7 %multiply_add_fusion.5 = f32[2,4,5,96,128]{4,3,2,1,0:T(8,128)S(1)} fusion(f32[2,4,5,96,128]{4,3,2,1,0:T(8,128)S(1)} %get-tuple-element.700, bf16[2,256,4,128,1]{1,3,4,2,0:T(8,128)(2,1)S(1)} %bitcast.89, f32[2,4,256,96,5]{2,3,4,1,0:T(8,128)} %copy-done.1, f32[2,4,5,96]{3,2,1,0:T(8,128)S(1)} %max.19, pred[2,96,256]{2,1,0:T(8,128)(4,1)S(1)} %copy-done.2, ...), kind=kOutput, calls=%fused_computation.7.clone.1 | convolution fusion | flops 256573440 | bytes 8468480 | tf_op jit(solution)/shard_map/while/body/eval_jaxpr/chgrn,cnhd->chgrd/dot_general | solution.py:42
  209.7 1.3 divide_bitcast_fusion
  212.4 1.2 select_convert_fusion
  218.0 27.5 %all-gather.11.cloned.1.call-done = bf16[8,96,2560]{2,1,0:T(8,128)(2,1)} async-done(((bf16[2,96,2560]{2,1,0:T(8,128)(2,1)}), bf16[8,96,2560]{2,1,0:T(8,128)(2,1)}) %all-gather.11.cloned.1.call-update) | async-done | bytes 3932176 | tf_op jit(solution)/shard_map/all_gather | solution.py:151
  245.6 1.2 constant_dynamic-slice_fusion.5
  (141 shorter events, 27.0 us)
Async XLA Ops:
  6.5 46.0 %copy-start.7 = (bf16[2,96,512]{2,1,0:T(8,128)(2,1)S(1)}, bf16[2,96,512]{2,1,0:T(8,128)(2,1)}, u32[]{:S(2)}) copy-start(bf16[2,96,512]{2,1,0:T(8,128)(2,1)} %param.14) | copy-start | bytes 589828
  6.5 47.0 %copy-start.6 = (bf16[2,96,2560]{2,1,0:T(8,128)(2,1)S(1)}, bf16[2,96,2560]{2,1,0:T(8,128)(2,1)}, u32[]{:S(2)}) copy-start(bf16[2,96,2560]{2,1,0:T(8,128)(2,1)} %param.12) | copy-start | bytes 2949124
  6.5 85.1 %all-gather.5.cloned.1.call-start = ((), (), s32[]{:S(2)}) async-start(), calls=%async_computation | async-start | bytes 2162688 | tf_op jit(solution)/shard_map/all_gather | solution.py:106
  7.3 152.0 %all-gather.7.cloned.1.call-start = ((), (), s32[]{:S(2)}) async-start(), calls=%async_computation.1 | async-start | bytes 1769472 | tf_op jit(solution)/shard_map/all_gather | solution.py:135
  9.1 158.7 %all-gather.9.cloned.1.call-start = ((), (), s32[]{:S(2)}) async-start(), calls=%async_computation.2 | async-start | bytes 1769472 | tf_op jit(solution)/shard_map/all_gather | solution.py:136
  10.1 9.4 %collective-permute-start = (bf16[64,512]{0,1:T(8,128)(2,1)S(1)}, bf16[64,512]{0,1:T(8,128)(2,1)S(1)}, u32[]{:S(2)}, u32[]{:S(2)}) collective-permute-start(bf16[64,512]{0,1:T(8,128)(2,1)S(1)} %copy.70), channel_id=1, source_target_pairs={{0,31},{1,0},{2,1},{3,2},{4,3},{5,4},{6,5},{7,6},{8,7},{9,8},{10,9... | collective-permute-start | bytes 196616 | tf_op jit(solution)/shard_map/ppermute | solution.py:101
  19.6 5.1 %collective-permute-start.1 = (bf16[128,512]{0,1:T(8,128)(2,1)S(1)}, bf16[128,512]{0,1:T(8,128)(2,1)S(1)}, u32[]{:S(2)}, u32[]{:S(2)}) collective-permute-start(bf16[128,512]{0,1:T(8,128)(2,1)S(1)} %pad_maximum_fusion.3), channel_id=1, source_target_pairs={{0,30},{1,31},{2,0},{3,1},{4,2},{5,3},{6,4},{7,5},{8,6},{9,7},{10,... | collective-permute-start | bytes 393224 | tf_op jit(solution)/shard_map/ppermute | solution.py:101
  24.9 15.4 %collective-permute-start.2 = (bf16[256,512]{0,1:T(8,128)(2,1)S(1)}, bf16[256,512]{0,1:T(8,128)(2,1)S(1)}, u32[]{:S(2)}, u32[]{:S(2)}) collective-permute-start(bf16[256,512]{0,1:T(8,128)(2,1)S(1)} %pad_maximum_fusion.2), channel_id=1, source_target_pairs={{0,28},{1,29},{2,30},{3,31},{4,0},{5,1},{6,2},{7,3},{8,4},{9,5},{1... | collective-permute-start | bytes 786440 | tf_op jit(solution)/shard_map/ppermute | solution.py:101
  40.5 8.7 %collective-permute-start.3 = (bf16[512,512]{0,1:T(8,128)(2,1)S(1)}, bf16[512,512]{0,1:T(8,128)(2,1)S(1)}, u32[]{:S(2)}, u32[]{:S(2)}) collective-permute-start(bf16[512,512]{0,1:T(8,128)(2,1)S(1)} %pad_maximum_fusion.1), channel_id=1, source_target_pairs={{0,24},{1,25},{2,26},{3,27},{4,28},{5,29},{6,30},{7,31},{8,0},{9,1... | collective-permute-start | bytes 1572872 | tf_op jit(solution)/shard_map/ppermute | solution.py:101
  51.1 5.3 %copy-start.9 = (s32[8]{0:T(128)S(1)}, s32[8]{0:T(128)}, u32[]{:S(2)}) copy-start(s32[8]{0:T(128)} %param.18) | copy-start | bytes 100
  51.1 5.4 %copy-start.10 = (s32[8]{0:T(128)S(1)}, s32[8]{0:T(128)}, u32[]{:S(2)}) copy-start(s32[8]{0:T(128)} %param.17) | copy-start | bytes 100
  51.1 28.8 %collective-permute-start.4 = (bf16[1024,512]{0,1:T(8,128)(2,1)}, bf16[1024,512]{0,1:T(8,128)(2,1)}, u32[]{:S(2)}, u32[]{:S(2)}) collective-permute-start(bf16[1024,512]{0,1:T(8,128)(2,1)} %concatenate.25), channel_id=1, source_target_pairs={{0,16},{1,17},{2,18},{3,19},{4,20},{5,21},{6,22},{7,23},{8,24},{9,... | collective-permute-start | bytes 3145736 | tf_op jit(solution)/shard_map/ppermute | solution.py:101
  53.5 192.1 %all-gather.11.cloned.1.call-start = ((), (), s32[]{:S(2)}) async-start(), calls=%async_computation.3 | async-start | bytes 4915200 | tf_op jit(solution)/shard_map/all_gather | solution.py:151
  97.3 5.7 %copy-start = (f32[4,512,2,96,5]{1,3,4,2,0:T(8,128)S(1)}, f32[4,512,2,96,5]{1,3,4,2,0:T(8,128)}, u32[]{:S(2)}) copy-start(f32[4,512,2,96,5]{1,3,4,2,0:T(8,128)} %get-tuple-element.641) | copy-start | bytes 23592964 | tf_op jit(solution)/shard_map/while
  112.3 5.7 %copy-start = (f32[4,512,2,96,5]{1,3,4,2,0:T(8,128)S(1)}, f32[4,512,2,96,5]{1,3,4,2,0:T(8,128)}, u32[]{:S(2)}) copy-start(f32[4,512,2,96,5]{1,3,4,2,0:T(8,128)} %get-tuple-element.641) | copy-start | bytes 23592964 | tf_op jit(solution)/shard_map/while
  128.8 5.8 %copy-start = (f32[4,512,2,96,5]{1,3,4,2,0:T(8,128)S(1)}, f32[4,512,2,96,5]{1,3,4,2,0:T(8,128)}, u32[]{:S(2)}) copy-start(f32[4,512,2,96,5]{1,3,4,2,0:T(8,128)} %get-tuple-element.641) | copy-start | bytes 23592964 | tf_op jit(solution)/shard_map/while
  145.4 5.8 %copy-start = (f32[4,512,2,96,5]{1,3,4,2,0:T(8,128)S(1)}, f32[4,512,2,96,5]{1,3,4,2,0:T(8,128)}, u32[]{:S(2)}) copy-start(f32[4,512,2,96,5]{1,3,4,2,0:T(8,128)} %get-tuple-element.641) | copy-start | bytes 23592964 | tf_op jit(solution)/shard_map/while
  171.2 2.2 copy-start.3
  171.2 4.1 %copy-start.2 = (pred[2,96,256]{2,1,0:T(8,128)(4,1)S(1)}, pred[2,96,256]{2,1,0:T(8,128)(4,1)}, u32[]{:S(2)}) copy-start(pred[2,96,256]{2,1,0:T(8,128)(4,1)} %broadcast_and_fusion.2) | copy-start | bytes 147460 | tf_op jit(solution)/shard_map/while
  171.2 5.6 %copy-start.4 = (f32[2,4,5,96]{3,2,1,0:T(8,128)S(1)}, f32[2,4,5,96]{3,2,1,0:T(8,128)}, u32[]{:S(2)}) copy-start(f32[2,4,5,96]{3,2,1,0:T(8,128)} %get-tuple-element.699) | copy-start | bytes 46084 | tf_op jit(solution)/shard_map/while
  173.5 1.9 copy-start.1
  176.9 4.3 %copy-start.5 = (f32[2,4,5,96]{3,2,1,0:T(8,128)}, f32[2,4,5,96]{3,2,1,0:T(8,128)S(1)}, u32[]{:S(2)}) copy-start(f32[2,4,5,96]{3,2,1,0:T(8,128)S(1)} %get-tuple-element.713) | copy-start | bytes 46084 | tf_op jit(solution)/shard_map/while
  185.1 2.2 copy-start.3
  185.2 4.1 %copy-start.2 = (pred[2,96,256]{2,1,0:T(8,128)(4,1)S(1)}, pred[2,96,256]{2,1,0:T(8,128)(4,1)}, u32[]{:S(2)}) copy-start(pred[2,96,256]{2,1,0:T(8,128)(4,1)} %broadcast_and_fusion.2) | copy-start | bytes 147460 | tf_op jit(solution)/shard_map/while
  185.2 5.6 %copy-start.4 = (f32[2,4,5,96]{3,2,1,0:T(8,128)S(1)}, f32[2,4,5,96]{3,2,1,0:T(8,128)}, u32[]{:S(2)}) copy-start(f32[2,4,5,96]{3,2,1,0:T(8,128)} %get-tuple-element.699) | copy-start | bytes 46084 | tf_op jit(solution)/shard_map/while
  187.4 1.9 copy-start.1
  190.8 4.3 %copy-start.5 = (f32[2,4,5,96]{3,2,1,0:T(8,128)}, f32[2,4,5,96]{3,2,1,0:T(8,128)S(1)}, u32[]{:S(2)}) copy-start(f32[2,4,5,96]{3,2,1,0:T(8,128)S(1)} %get-tuple-element.713) | copy-start | bytes 46084 | tf_op jit(solution)/shard_map/while
  199.1 2.2 copy-start.3
  199.1 4.1 %copy-start.2 = (pred[2,96,256]{2,1,0:T(8,128)(4,1)S(1)}, pred[2,96,256]{2,1,0:T(8,128)(4,1)}, u32[]{:S(2)}) copy-start(pred[2,96,256]{2,1,0:T(8,128)(4,1)} %broadcast_and_fusion.2) | copy-start | bytes 147460 | tf_op jit(solution)/shard_map/while
  199.1 5.6 %copy-start.4 = (f32[2,4,5,96]{3,2,1,0:T(8,128)S(1)}, f32[2,4,5,96]{3,2,1,0:T(8,128)}, u32[]{:S(2)}) copy-start(f32[2,4,5,96]{3,2,1,0:T(8,128)} %get-tuple-element.699) | copy-start | bytes 46084 | tf_op jit(solution)/shard_map/while
  201.3 1.9 copy-start.1
  204.8 4.3 %copy-start.5 = (f32[2,4,5,96]{3,2,1,0:T(8,128)}, f32[2,4,5,96]{3,2,1,0:T(8,128)S(1)}, u32[]{:S(2)}) copy-start(f32[2,4,5,96]{3,2,1,0:T(8,128)S(1)} %get-tuple-element.713) | copy-start | bytes 46084 | tf_op jit(solution)/shard_map/while
  211.0 2.6 %copy-start.8 = (s32[8]{0:T(128)S(1)}, s32[8]{0:T(128)}, u32[]{:S(2)}) copy-start(s32[8]{0:T(128)} %param.19) | copy-start | bytes 100
Sparse Core Ops, SparseCore 0:
  10.3 66.9 all-gather.4
  79.5 43.0 all-gather.6
  124.8 42.9 all-gather.8
  213.7 31.7 all-gather.10
